TPU v7x, 32 devices: a whole 2x2x4 slice. The times are simulated.
32 devices in a mesh: head: 2 (over y), tm: 16 (over z, x, core).
Axes of the slice: x: 2, y: 2, z: 4, core: 2. Of those that a mesh axis runs over, the one named last changes fastest.
Arguments:
- frames: bfloat16 [16384, 1024], P('tm'), may hold values from -6 to 6
- segment_lengths: int32 [128], replicated, may hold values from 1 to 512, 16384 in all
- attn_gain: float32 [1024], replicated, may hold values from 0.5 to 1.5
- qkv_proj: bfloat16 [1024, 3, 1024], P('tm', None, 'head'), may hold values from -0.1875 to 0.1875
- out_proj: bfloat16 [1024, 1024], P(None, 'tm'), may hold values from -0.1875 to 0.1875
- logit_scale: float32 [16], P('head'), may hold values from 2 to 16
- conv_gain: float32 [1024], replicated, may hold values from 0.5 to 1.5
- glu_proj: bfloat16 [1024, 2048], P('tm'), may hold values from -0.1875 to 0.1875
- kernel: float32 [31, 1024], replicated, may hold values from -1 to 1
- post_gain: float32 [1024], replicated, may hold values from 0.5 to 1.5
- mix_proj: bfloat16 [1024, 1024], P('tm'), may hold values from -0.1875 to 0.1875
- cotangent: bfloat16 [16384, 1024], P('tm', 'head'), may hold values from -6 to 6
Outputs:
- out_frames: bfloat16 [16384, 1024], P('tm', 'head')
- grad_input: bfloat16 [16384, 1024], P('tm', 'head')
- grad_kernel: float32 [31, 1024], replicated
- grad_gains: float32 [2, 1024], replicated
Inputs may be any that keep to these rules, and one draw needn't show every extreme that they name: `segment_lengths`: the 128 lengths sum to 16384; the longest is exactly 512 frames.
All inputs are finite; a program needn't handle non-finite values.
Results may differ from a plain program's by a relative error of at most 0.014.
Values may be sent and summed in bfloat16 or wider, within the bound.
No kernel may reach another device: no remote copies, remote signals or barrier semaphores. Data moves between devices by JAX's collectives and lax.ppermute only.
A program may use at most 128 MiB of HBM per device.

v0:
```python
import math
import jax
import jax.numpy as jnp
from jax import lax
from jax.sharding import PartitionSpec as P

HD = 64
KERNEL = 31
HALF = 15
MOST = 512
EPS_NORM = 1e-05
EPS_HEAD = 1e-06


def extended(cells, sides, width, closed):
    for axis, dim in sides:
        count = lax.axis_size(axis)
        ends = count if closed else count - 1
        head = lax.slice_in_dim(cells, 0, width, axis=dim)
        tail = lax.slice_in_dim(cells, cells.shape[dim] - width, cells.shape[dim], axis=dim)
        cells = jnp.concatenate(
            [
                lax.ppermute(tail, axis, [(i, (i + 1) % count) for i in range(ends)]),
                cells,
                lax.ppermute(head, axis, [((i + 1) % count, i) for i in range(ends)]),
            ],
            axis=dim,
        )
    return cells


def layer_stats(values):
    average = jnp.mean(values, axis=-1, keepdims=True)
    centred = values - average
    inverse = lax.rsqrt(jnp.mean(centred * centred, axis=-1, keepdims=True) + EPS_NORM)
    return (centred * inverse, inverse)


def unit_heads(values):
    return values * lax.rsqrt(jnp.mean(values * values, axis=-1, keepdims=True) + EPS_HEAD)


def norm_back(gradient, normed, inverse, gain):
    scaled = gradient * gain
    return inverse * (
        scaled
        - jnp.mean(scaled, axis=-1, keepdims=True)
        - normed * jnp.mean(scaled * normed, axis=-1, keepdims=True)
    )


def on_device(
    frames,
    segment_lengths,
    attn_gain,
    qkv_proj,
    out_proj,
    logit_scale,
    conv_gain,
    glu_proj,
    kernel,
    post_gain,
    mix_proj,
    cotangent,
):
    head_count = lax.axis_size("head")
    shard_count = lax.axis_size("tm")
    head_place = lax.axis_index("head")
    shard_place = lax.axis_index("tm")
    local_frames = frames.shape[0]
    model_width = frames.shape[1]
    conv_rows = local_frames // head_count
    local_width = qkv_proj.shape[2]
    local_heads = local_width // HD
    all_frames = local_frames * shard_count
    segment_ends = jnp.cumsum(segment_lengths)

    def segment_of(positions):
        located = jnp.sum((segment_ends[None, :] <= positions[:, None]).astype(jnp.int32), axis=1)
        return jnp.where(positions < 0, -1, located)

    own_rows = lax.dynamic_slice_in_dim(out_proj, head_place * local_width, local_width, 0)
    qkv_weight, out_weight = (
        lax.all_gather(qkv_proj, "tm", axis=0, tiled=True),
        lax.all_gather(own_rows, "tm", axis=1, tiled=True),
    )
    glu_weight, proj_weight = (
        lax.all_gather(glu_proj, "tm", axis=0, tiled=True),
        lax.all_gather(mix_proj, "tm", axis=0, tiled=True),
    )
    frame_float = frames.astype(jnp.float32)
    attn_normed = (layer_stats(frame_float)[0] * attn_gain).astype(jnp.bfloat16)
    projected = jnp.dot(
        attn_normed,
        qkv_weight.reshape(model_width, 3 * local_width),
        preferred_element_type=jnp.float32,
    )
    query_heads = unit_heads(
        projected[:, :local_width].reshape(local_frames, local_heads, HD)
    ).astype(jnp.bfloat16)
    key_heads = unit_heads(
        projected[:, local_width : 2 * local_width].reshape(local_frames, local_heads, HD)
    ).astype(jnp.bfloat16)
    value_heads = projected[:, 2 * local_width :].astype(jnp.bfloat16)
    key_value = jnp.stack([key_heads.reshape(local_frames, local_width), value_heads], axis=1)
    key_padded = extended(key_value, (("tm", 0),), MOST, False)
    key_segment = segment_of(
        shard_place * local_frames - MOST + jnp.arange(local_frames + 2 * MOST, dtype=jnp.int32)
    )
    query_block = min(512, local_frames)
    factor = (logit_scale / HD)[:, None, None]

    def attend(row_start, query_rows, key_start, key_span):
        key_rows = lax.dynamic_slice_in_dim(key_padded, key_start, key_span, 0)
        query_seg = lax.dynamic_slice_in_dim(key_segment, row_start + MOST, query_block, 0)
        key_seg = lax.dynamic_slice_in_dim(key_segment, key_start, key_span, 0)
        key_part = key_rows[:, 0].reshape(key_span, local_heads, HD)
        value_part = key_rows[:, 1].reshape(key_span, local_heads, HD)
        scores = (
            jnp.einsum("qhd,khd->hqk", query_rows, key_part, preferred_element_type=jnp.float32)
            * factor
        )
        weights = jnp.where((query_seg[:, None] == key_seg[None, :])[None], jnp.exp(scores), 0.0)
        weights = (weights / jnp.sum(weights, axis=-1, keepdims=True)).astype(jnp.bfloat16)
        mixed_heads = jnp.einsum(
            "hqk,khd->qhd", weights, value_part, preferred_element_type=jnp.float32
        )
        return mixed_heads.astype(jnp.bfloat16).reshape(query_block, local_width)

    def attend_block(block_index):
        row_start = block_index * query_block
        query_rows = lax.dynamic_slice_in_dim(query_heads, row_start, query_block, 0)
        return attend(row_start, query_rows, row_start, query_block + 2 * MOST)

    heads_out = lax.map(
        attend_block, jnp.arange(local_frames // query_block, dtype=jnp.int32)
    ).reshape(local_frames, local_width)
    attn_rows = lax.psum_scatter(
        jnp.dot(heads_out, out_weight, preferred_element_type=jnp.float32).astype(jnp.bfloat16),
        "head",
        scatter_dimension=0,
        tiled=True,
    ).astype(jnp.float32)
    frame_rows = lax.dynamic_slice_in_dim(frame_float, head_place * conv_rows, conv_rows, 0)
    residual = (frame_rows + attn_rows).astype(jnp.bfloat16)
    residual_float = residual.astype(jnp.float32)
    conv_normed, conv_inverse = layer_stats(residual_float)
    conv_input = (conv_normed * conv_gain).astype(jnp.bfloat16)
    glu_linear = jnp.dot(conv_input, glu_weight, preferred_element_type=jnp.float32)
    glu_value = glu_linear[:, :model_width]
    gate_sigmoid = jax.nn.sigmoid(glu_linear[:, model_width:])
    gated = (glu_value * gate_sigmoid).astype(jnp.bfloat16)

    def with_rims(block_rows):
        beside_all = extended(block_rows, (("head", 0),), HALF, True)
        outer_rims = jnp.concatenate([beside_all[-HALF:], beside_all[:HALF]], 0)
        beyond = extended(outer_rims, (("tm", 0),), HALF, False)
        left_rim = jnp.where(head_place == 0, beyond[:HALF], beside_all[:HALF])
        right_rim = jnp.where(head_place == head_count - 1, beyond[-HALF:], beside_all[-HALF:])
        return jnp.concatenate([left_rim, block_rows, right_rim], 0)

    gated_padded = with_rims(gated)
    conv_start = (shard_place * head_count + head_place) * conv_rows
    conv_segment = segment_of(conv_start - HALF + jnp.arange(conv_rows + 2 * HALF, dtype=jnp.int32))
    window_index = jnp.arange(conv_rows)[:, None] + jnp.arange(KERNEL)[None, :]
    mask_table = (
        conv_segment[window_index] == conv_segment[HALF : HALF + conv_rows][:, None]
    ).astype(jnp.float32)

    def depthwise(padded, tap_weights):
        summed = jnp.zeros((conv_rows, model_width), jnp.float32)
        for offset in range(KERNEL):
            summed = (
                summed
                + tap_weights[offset]
                * padded[offset : offset + conv_rows].astype(jnp.float32)
                * mask_table[:, offset : offset + 1]
            )
        return summed

    depth_out = depthwise(gated_padded, kernel)
    post_normed, post_inverse = layer_stats(depth_out)
    post_scaled = post_normed * post_gain
    post_sigmoid = jax.nn.sigmoid(post_scaled)
    swished = (post_scaled * post_sigmoid).astype(jnp.bfloat16)
    out_rows = (
        residual_float + jnp.dot(swished, proj_weight, preferred_element_type=jnp.float32)
    ).astype(jnp.bfloat16)
    out_frames = lax.all_to_all(out_rows, "head", split_axis=1, concat_axis=0, tiled=True)
    upstream = lax.all_to_all(cotangent, "head", split_axis=0, concat_axis=1, tiled=True)
    swish_grad = jnp.dot(upstream, proj_weight.T, preferred_element_type=jnp.float32)
    post_grad = swish_grad * (post_sigmoid * (1.0 + post_scaled * (1.0 - post_sigmoid)))
    depth_grad = norm_back(post_grad, post_normed, post_inverse, post_gain).astype(jnp.bfloat16)
    gated_grad = depthwise(with_rims(depth_grad), kernel[::-1])
    depth_float = depth_grad.astype(jnp.float32)
    kernel_terms = jnp.stack(
        [
            jnp.sum(
                depth_float
                * gated_padded[offset : offset + conv_rows].astype(jnp.float32)
                * mask_table[:, offset : offset + 1],
                axis=0,
            )
            for offset in range(KERNEL)
        ],
        0,
    )
    glu_grad = jnp.concatenate(
        [gated_grad * gate_sigmoid, gated_grad * glu_value * gate_sigmoid * (1.0 - gate_sigmoid)], 1
    ).astype(jnp.bfloat16)
    input_grad = jnp.dot(glu_grad, glu_weight.T, preferred_element_type=jnp.float32)
    residual_grad = (
        upstream.astype(jnp.float32) + norm_back(input_grad, conv_normed, conv_inverse, conv_gain)
    ).astype(jnp.bfloat16)
    gain_terms = jnp.stack(
        [jnp.sum(input_grad * conv_normed, axis=0), jnp.sum(post_grad * post_normed, axis=0)], 0
    )
    kernel_sum, gain_sum = lax.psum((kernel_terms, gain_terms), ("head", "tm"))
    grad_scale = 1.0 / math.sqrt(all_frames)
    grad_input = lax.all_to_all(residual_grad, "head", split_axis=1, concat_axis=0, tiled=True)
    return (out_frames, grad_input, kernel_sum * grad_scale, gain_sum * grad_scale)


def solution(mesh):
    placed = (
        P("tm", None),
        P(),
        P(),
        P("tm", None, "head"),
        P(None, "tm"),
        P("head"),
        P(),
        P("tm", None),
        P(),
        P(),
        P("tm", None),
        P("tm", "head"),
    )
    return jax.shard_map(
        on_device,
        mesh=mesh,
        in_specs=placed,
        out_specs=(P("tm", "head"), P("tm", "head"), P(), P()),
        check_vma=False,
    )
```

profile of v0, /device:TPU:0, one launch (start us, length us, event | category | flops | bytes accessed | tf_op | source)
XLA Modules:
  0.0 488.0 jit_solution(7400596972553521557)
XLA Ops:
  11.9 46.5 %all-gather.5.cloned.1.call-done = bf16[1024,3,512]{2,0,1:T(8,128)(2,1)} async-done(((bf16[64,3,512]{2,0,1:T(8,128)(2,1)}), bf16[1024,3,512]{2,0,1:T(8,128)(2,1)}) %all-gather.5.cloned.1.call-update) | async-done | bytes 3145744 | tf_op jit(solution)/shard_map/all_gather | solution.py:84
  58.5 4.7 copy.43
  63.2 5.4 %fusion.83 = f32[1024,1536]{1,0:T(8,128)S(1)} fusion(bf16[1024,1536]{0,1:T(8,128)(2,1)} %bitcast.141, bf16[1024,1024]{1,0:T(8,128)(2,1)S(1)} %copy-done.4, f32[1024]{0:T(1024)S(1)} %copy-done.32, f32[1024]{0:T(1024)S(1)} %add_rsqrt_fusion.2, f32[1024]{0:T(1024)S(1)} %broadcast_multiply_fusion.2), kind=kOutput, calls=%fused_computation.216 | convolution fusion | flops 3226468352 | bytes 11546624 | tf_op jit(solution)/shard_map/dot_general | solution.py:93
  77.2 4.7 fusion.246
  95.6 65.1 %while.12 = (s32[]{:T(128)}, bf16[2,512,512]{2,1,0:T(8,128)(2,1)}, s32[2]{0:T(128)S(1)}, bf16[2048,2,512]{2,0,1:T(8,128)(2,1)}, s32[2048]{0:T(1024)S(1)}, /*inde...) while((s32[]{:T(128)}, bf16[2,512,512]{2,1,0:T(8,128)(2,1)}, ...), condition=%wide.region_8.9_spmd, body=%wide.region_6.8_spmd.sunk | while | flops 1655697408 | bytes 71623536 | solution.py:135
  102.1 13.1 %fusion.267 = (f32[8,512]{1,0:T(8,128)S(1)}, f32[8,512,1536]{2,1,0:T(8,128)}) fusion(f32[8]{0:T(128)S(1)} %bitcast.241, pred[512,1536]{1,0:T(8,128)(4,1)} %broadcast_compare_fusion.2, bf16[1536,8,64]{0,2,1:T(8,128)(2,1)} %bitcast.130, bf16[1024,8,64]{0,2,1:T(8,128)(2,1)} %get-tuple-element.344, s32[]{:T(128)S(6)} %select_n.108), kind=kOutput, calls=%fused_computation.3.clone.1 | convolution fusion | flops 824176640 | bytes 28065828 | tf_op jit(solution)/shard_map/while/body/eval_jaxpr/qhd,khd->hqk/dot_general | solution.py:120
  115.9 11.2 %fusion.268 = bf16[8,64,512]{2,1,0:T(8,128)(2,1)S(1)} fusion(bf16[1536,8,64]{0,2,1:T(8,128)(2,1)S(1)} %bitcast.131, f32[8,512,1536]{2,1,0:T(8,128)} %get-tuple-element.307, f32[8,512]{1,0:T(8,128)S(1)} %get-tuple-element.308, f32[8]{0:T(128)S(1)} %bitcast.242, pred[512,1536]{1,0:T(8,128)(4,1)} %broadcast_compare_fusion.2), kind=kOutput, calls=%fused_computation.6.clone.1 | convolution fusion | flops 830734336 | bytes 28065824 | tf_op jit(solution)/shard_map/while/body/eval_jaxpr/hqk,khd->qhd/dot_general | solution.py:125
  134.7 13.1 %fusion.267 = (f32[8,512]{1,0:T(8,128)S(1)}, f32[8,512,1536]{2,1,0:T(8,128)}) fusion(f32[8]{0:T(128)S(1)} %bitcast.241, pred[512,1536]{1,0:T(8,128)(4,1)} %broadcast_compare_fusion.2, bf16[1536,8,64]{0,2,1:T(8,128)(2,1)} %bitcast.130, bf16[1024,8,64]{0,2,1:T(8,128)(2,1)} %get-tuple-element.344, s32[]{:T(128)S(6)} %select_n.108), kind=kOutput, calls=%fused_computation.3.clone.1 | convolution fusion | flops 824176640 | bytes 28065828 | tf_op jit(solution)/shard_map/while/body/eval_jaxpr/qhd,khd->hqk/dot_general | solution.py:120
  148.4 11.2 %fusion.268 = bf16[8,64,512]{2,1,0:T(8,128)(2,1)S(1)} fusion(bf16[1536,8,64]{0,2,1:T(8,128)(2,1)S(1)} %bitcast.131, f32[8,512,1536]{2,1,0:T(8,128)} %get-tuple-element.307, f32[8,512]{1,0:T(8,128)S(1)} %get-tuple-element.308, f32[8]{0:T(128)S(1)} %bitcast.242, pred[512,1536]{1,0:T(8,128)(4,1)} %broadcast_compare_fusion.2), kind=kOutput, calls=%fused_computation.6.clone.1 | convolution fusion | flops 830734336 | bytes 28065824 | tf_op jit(solution)/shard_map/while/body/eval_jaxpr/hqk,khd->qhd/dot_general | solution.py:125
  160.7 4.1 convolution_convert_fusion
  165.4 3.7 all-to-all-start.1
  173.2 55.4 %gather_fusion = s32[15872]{0:T(1024)S(1)} fusion(s32[542]{0:T(1024)S(1)} %compare_select_fusion.2, s32[16384]{0:T(1024)S(1)} %pad_clamp_fusion), kind=kCustom, calls=%fused_computation | custom fusion | bytes 190464 | tf_op jit(solution)/shard_map/gather | solution.py:167
  231.9 40.1 %all-gather.9.cloned.1.call-done = bf16[1024,2048]{1,0:T(8,128)(2,1)} async-done(((bf16[64,2048]{1,0:T(8,128)(2,1)}), bf16[1024,2048]{1,0:T(8,128)(2,1)}) %all-gather.9.cloned.1.call-update) | async-done | bytes 4194320 | tf_op jit(solution)/shard_map/all_gather | solution.py:88
  272.0 4.6 fusion.176
  291.5 18.7 %fusion.244 = (f32[512]{0:T(512)S(1)}, f32[512,1024]{1,0:T(8,128)S(1)}) fusion(f32[512]{0:T(512)S(1)} %get-tuple-element.160, bf16[15,1024]{1,0:T(8,128)(2,1)S(1)} %broadcast_select_fusion.1, bf16[512,1024]{1,0:T(8,128)(2,1)S(1)} %multiply_convert_fusion.6, f32[1024]{0:T(1024)S(1)} %bitcast.202, f32[512]{0:T(512)S(1)} %get-tuple-element.161, ...), kind=kLoop, calls=%fused_computation.483 | loop fusion | flops 112197120 | bytes 3399680 | tf_op jit(solution)/shard_map/reduce_sum | solution.py:33
  314.0 4.7 multiply_reduce_fusion.1
  318.7 7.3 %fusion.160 = (f32[1024]{0:T(1024)}, f32[1024]{0:T(1024)}, f32[1024]{0:T(1024)}, f32[1024]{0:T(1024)}, f32[1024]{0:T(1024)}, /*index=5*/f32[1024]{0:T(1024)}, bf16[512,1024]{1,0:T(8,128)(2,1)S(1)}) fusion(f32[512]{0:T(512)S(1)} %get-tuple-element.161, bf16[15,1024]{1,0:T(8,128)(2,1)S(1)} %broadcast_select_fusion.1, ...), kind=kLoop, calls=%fused_computation.293 | loop fusion | flops 26732544 | bytes 6371328 | tf_op jit(solution)/shard_map/reduce_sum | solution.py:198
  326.1 6.9 %fusion.162 = (f32[1024]{0:T(1024)}, f32[1024]{0:T(1024)}, f32[1024]{0:T(1024)}, f32[1024]{0:T(1024)}, f32[1024]{0:T(1024)}, /*index=5*/f32[1024]{0:T(1024)}) fusion(bf16[512,1024]{1,0:T(8,128)(2,1)S(1)} %get-tuple-element.204, bf16[15,1024]{1,0:T(8,128)(2,1)S(1)} %broadcast_select_fusion.1, bf16[512,1024]{1,0:T(8,128)(2,1)S(1)} %multiply_convert_fusion.6, ...), kind=kLoop, calls=%fused_computation.295 | loop fusion | flops 22538240 | bytes 2164736 | tf_op jit(solution)/shard_map/reduce_sum | solution.py:198
  336.2 3.9 fusion.130
  340.0 4.1 fusion.128
  348.2 5.5 %stack.144 = f32[31,1024]{1,0:T(8,128)} concatenate(f32[1,1024]{1,0:T(1,128)} %bitcast.233, f32[1,1024]{1,0:T(1,128)} %bitcast.236, f32[1,1024]{1,0:T(1,128)} %bitcast.235, f32[1,1024]{1,0:T(1,128)} %bitcast.234, f32[1,1024]{1,0:T(1,128)} %bitcast.223, f32[1,1024]{1,0:T(1,128)} %bitcast.224, f32[1,1024]{1,0:T(1,128)} %bitcast.225, f32[1,1024]{1,0:T(1,128)} %bitcast.226, ...), dimensions={0} | concatenate | bytes 253952 | tf_op jit(solution)/shard_map/stack | solution.py:196
  367.4 19.0 %multiply_convert_fusion.3 = (bf16[512,1024]{1,0:T(8,128)(2,1)S(1)}, f32[512,1024]{1,0:T(8,128)S(1)}) fusion(f32[512,2048]{1,0:T(8,128)} %copy-done.2, f32[512]{0:T(512)S(1)} %get-tuple-element.160, bf16[15,1024]{1,0:T(8,128)(2,1)S(1)} %broadcast_select_fusion, bf16[512,1024]{1,0:T(8,128)(2,1)S(1)} %get-tuple-element.204, f32[1024]{0:T(1024)S(1)} %bitcast.145, ...), kind=kLoop, calls=%fused_computation.310 | loop fusion | flops 114294784 | bytes 6543360 | tf_op jit(solution)/shard_map/convert
  396.9 48.6 %psum.15 = f32[2,1024]{1,0:T(2,128)S(1)} all-reduce(f32[2,1024]{1,0:T(2,128)S(1)} %pad_maximum_fusion.6), channel_id=1, replica_groups=mesh['head'=2,'tm'=16] {'head','tm'}, use_global_device_ids=true, to_apply=%region_53.54 | all-reduce | flops 2048 | bytes 16384 | tf_op jit(solution)/shard_map/psum | solution.py:218
  446.2 31.3 %all-reduce.2.cloned.1.call-done = f32[31,1024]{1,0:T(8,128)} async-done(((f32[31,1024]{1,0:T(8,128)}), f32[31,1024]{1,0:T(8,128)}) %all-reduce.2.cloned.1.call-update) | async-done | bytes 126992 | tf_op jit(solution)/shard_map/psum | solution.py:218
  (198 shorter events, 103.6 us)
Async XLA Ops:
  7.2 51.3 %all-gather.5.cloned.1.call-start = ((), (), s32[]{:S(2)}) async-start(), calls=%async_computation.4 | async-start | bytes 3342336 | tf_op jit(solution)/shard_map/all_gather | solution.py:84
  7.9 152.8 %all-gather.7.cloned.1.call-start = ((), (), s32[]{:S(2)}) async-start(), calls=%async_computation.5 | async-start | bytes 1114112 | tf_op jit(solution)/shard_map/all_gather | solution.py:85
  8.7 220.3 %reduce-scatter.2.cloned.1.call-start = ((), (), s32[]{:S(2)}) async-start(), calls=%async_computation.6 | async-start | bytes 3145728 | tf_op jit(solution)/shard_map/reduce_scatter | solution.py:138
  11.9 76.1 %copy-start.24 = (s32[128]{0:T(128)}, s32[128]{0:T(128)S(1)}, u32[]{:S(2)}) copy-start(s32[128]{0:T(128)S(1)} %reduce) | copy-start | bytes 1540
  11.9 51.2 %copy-start.32 = (f32[1024]{0:T(1024)S(1)}, f32[1024]{0:T(1024)}, u32[]{:S(2)}) copy-start(f32[1024]{0:T(1024)} %param.16) | copy-start | bytes 12292
  83.4 8.8 %collective-permute-start = (bf16[512,2,512]{2,0,1:T(8,128)(2,1)}, bf16[512,2,512]{2,0,1:T(8,128)(2,1)}, u32[]{:S(2)}, u32[]{:S(2)}) collective-permute-start(bf16[512,2,512]{2,0,1:T(8,128)(2,1)} %get-tuple-element.217), channel_id=1, source_target_pairs={{0,1},{1,2},{2,3},{3,4},{4,5},{5,6},{6,7},{7,8},{8,9},{9,10},{10,1... | collective-permute-start | bytes 3145736 | tf_op jit(solution)/shard_map/ppermute | solution.py:23
  86.6 5.7 %collective-permute-start.1 = (bf16[512,2,512]{2,0,1:T(8,128)(2,1)}, bf16[512,2,512]{2,0,1:T(8,128)(2,1)}, u32[]{:S(2)}, u32[]{:S(2)}) collective-permute-start(bf16[512,2,512]{2,0,1:T(8,128)(2,1)} %get-tuple-element.218), channel_id=1, source_target_pairs={{1,0},{2,1},{3,2},{4,3},{5,4},{6,5},{7,6},{8,7},{9,8},{10,9},{11,1... | collective-permute-start | bytes 3145736 | tf_op jit(solution)/shard_map/ppermute | solution.py:25
  164.9 107.1 %all-gather.9.cloned.1.call-start = ((), (), s32[]{:S(2)}) async-start(), calls=%async_computation.7 | async-start | bytes 4456448 | tf_op jit(solution)/shard_map/all_gather | solution.py:88
  165.4 121.3 %all-to-all-start.1 = ((bf16[2,512,512]{2,1,0:T(8,128)(2,1)}), bf16[2,512,512]{2,1,0:T(8,128)(2,1)S(1)}, u32[]{:S(2)}, u32[]{:S(2)}) async-start(bf16[2,512,512]{2,1,0:T(8,128)(2,1)} %bitcast.142), calls=%async_computation.2 | async-start | bytes 2097152 | tf_op jit(solution)/shard_map/all_to_all | solution.py:190
  169.2 144.8 %all-gather.11.cloned.1.call-start = ((), (), s32[]{:S(2)}) async-start(), calls=%async_computation.8 | async-start | bytes 2228224 | tf_op jit(solution)/shard_map/all_gather | solution.py:89
  169.8 307.7 %all-reduce.2.cloned.1.call-start = ((), (), s32[]{:S(2)}) async-start(), calls=%async_computation.9 | async-start | bytes 262144 | tf_op jit(solution)/shard_map/psum | solution.py:218
  229.0 43.0 %copy-start.28 = (f32[1024]{0:T(1024)S(1)}, f32[1024]{0:T(1024)}, u32[]{:S(2)}) copy-start(f32[1024]{0:T(1024)} %param.20) | copy-start | bytes 12292
  231.4 45.2 %copy-start.18 = (f32[512]{0:T(512)}, f32[512]{0:T(512)S(1)}, u32[]{:S(2)}) copy-start(f32[512]{0:T(512)S(1)} %broadcast_multiply_fusion.8) | copy-start | bytes 6148
  231.9 44.8 %copy-start.21 = (f32[512]{0:T(512)}, f32[512]{0:T(512)S(1)}, u32[]{:S(2)}) copy-start(f32[512]{0:T(512)S(1)} %add_rsqrt_fusion.4) | copy-start | bytes 6148
  278.6 4.8 collective-permute-start.2
  282.8 5.1 %collective-permute-start.4 = (bf16[15,1024]{1,0:T(8,128)(2,1)S(1)}, bf16[15,1024]{1,0:T(8,128)(2,1)S(1)}, u32[]{:S(2)}, u32[]{:S(2)}) collective-permute-start(bf16[15,1024]{1,0:T(8,128)(2,1)S(1)} %get-tuple-element.222), channel_id=1, source_target_pairs={{16,0},{0,16},{17,1},{1,17},{18,2},{2,18},{19,3},{3,19},{20,4},{4,... | collective-permute-start | bytes 92168 | tf_op jit(solution)/shard_map/ppermute | solution.py:25
  283.4 6.2 %collective-permute-start.3 = (bf16[15,1024]{1,0:T(8,128)(2,1)S(1)}, bf16[15,1024]{1,0:T(8,128)(2,1)S(1)}, u32[]{:S(2)}, u32[]{:S(2)}) collective-permute-start(bf16[15,1024]{1,0:T(8,128)(2,1)S(1)} %collective-permute-done.2), channel_id=1, source_target_pairs={{0,1},{1,2},{2,3},{3,4},{4,5},{5,6},{6,7},{7,8},{8,9},{9,10},{10,1... | collective-permute-start | bytes 92168 | tf_op jit(solution)/shard_map/ppermute | solution.py:23
  287.9 3.6 collective-permute-start.5
  344.2 9.6 %collective-permute-start.6 = (bf16[15,1024]{1,0:T(8,128)(2,1)S(1)}, bf16[15,1024]{1,0:T(8,128)(2,1)S(1)}, u32[]{:S(2)}, u32[]{:S(2)}) collective-permute-start(bf16[15,1024]{1,0:T(8,128)(2,1)S(1)} %get-tuple-element.219), channel_id=1, source_target_pairs={{0,16},{16,0},{1,17},{17,1},{2,18},{18,2},{3,19},{19,3},{4,20},{20... | collective-permute-start | bytes 92168 | tf_op jit(solution)/shard_map/ppermute | solution.py:23
  347.7 16.0 %collective-permute-start.8 = (bf16[15,1024]{1,0:T(8,128)(2,1)S(1)}, bf16[15,1024]{1,0:T(8,128)(2,1)S(1)}, u32[]{:S(2)}, u32[]{:S(2)}) collective-permute-start(bf16[15,1024]{1,0:T(8,128)(2,1)S(1)} %get-tuple-element.220), channel_id=1, source_target_pairs={{16,0},{0,16},{17,1},{1,17},{18,2},{2,18},{19,3},{3,19},{20,4},{4,... | collective-permute-start | bytes 92168 | tf_op jit(solution)/shard_map/ppermute | solution.py:25
  353.8 11.2 %collective-permute-start.7 = (bf16[15,1024]{1,0:T(8,128)(2,1)S(1)}, bf16[15,1024]{1,0:T(8,128)(2,1)S(1)}, u32[]{:S(2)}, u32[]{:S(2)}) collective-permute-start(bf16[15,1024]{1,0:T(8,128)(2,1)S(1)} %collective-permute-done.6), channel_id=1, source_target_pairs={{0,1},{1,2},{2,3},{3,4},{4,5},{5,6},{6,7},{7,8},{8,9},{9,10},{10,1... | collective-permute-start | bytes 92168 | tf_op jit(solution)/shard_map/ppermute | solution.py:23
  360.1 33.2 %all-to-all-start = ((bf16[512,2,512]{2,0,1:T(8,128)(2,1)}), bf16[512,2,512]{2,0,1:T(8,128)(2,1)S(1)}, u32[]{:S(2)}, u32[]{:S(2)}) async-start(bf16[512,2,512]{2,0,1:T(8,128)(2,1)} %bitcast.136), calls=%async_computation.1 | async-start | bytes 2097152 | tf_op jit(solution)/shard_map/all_to_all | solution.py:189
  363.7 3.7 collective-permute-start.9
  393.3 85.7 %all-to-all-start.2 = ((bf16[512,2,512]{2,0,1:T(8,128)(2,1)}), bf16[512,2,512]{2,0,1:T(8,128)(2,1)S(1)}, u32[]{:S(2)}, u32[]{:S(2)}) async-start(bf16[512,2,512]{2,0,1:T(8,128)(2,1)} %bitcast.114), calls=%async_computation.3 | async-start | bytes 2097152 | tf_op jit(solution)/shard_map/all_to_all | solution.py:220
  (29 other events, 241.7 us)
Sparse Core Ops, SparseCore 0:
  10.2 48.2 all-gather.4
  61.2 36.9 all-gather.6
  165.0 53.5 reduce-scatter.1
  220.6 51.3 all-gather.8
  274.0 39.9 all-gather.10
  353.9 123.4 all-reduce.1
where the time goes:
time: 494 us; the launch traced here: 488 us
  waiting for transfers between devices  127 us (26%)
  local copies, waits for them, and re-layouts  100 us (20%)
  other arithmetic  95.2 us (19%)
  matrix products  73.9 us (15%)
  blocking collectives  48.6 us (10%)
  starting transfers between devices  26.2 us (5%)
  between operations  15.1 us (3%)
    gather x2, local copies, waits for them, and re-layouts, on_device(): conv_segment[window_index] == conv_segment[HALF:HALF + conv_rows][:, None]  55.6 us
    psum x1, blocking collectives, on_device(): kernel_sum, gain_sum = lax.psum((kernel_terms, gain_terms), ('head', 'tm'))  48.6 us
    all_gather x1, waiting for transfers between devices, on_device(): lax.all_gather(qkv_proj, 'tm', axis=0, tiled=True)  46.5 us
    all_gather x1, waiting for transfers between devices, on_device(): lax.all_gather(glu_proj, 'tm', axis=0, tiled=True)  40.1 us
    psum x1, waiting for transfers between devices, on_device(): kernel_sum, gain_sum = lax.psum((kernel_terms, gain_terms), ('head', 'tm'))  31.3 us
    reduce_sum x6, other arithmetic, on_device(): jnp.sum(depth_float * gated_padded[offset:offset + conv_rows].astype(jnp....  27.4 us
    dot_general x2, matrix products, attend(): jnp.einsum('qhd,khd->hqk', query_rows, key_part, preferred_element_type=j...  26.2 us
    reduce_sum x3, other arithmetic, layer_stats(): average = jnp.mean(values, axis=-1, keepdims=True)  22.9 us
  transfers between devices with their start and end apart: 19, of which 6 were waited for; matrix products, arithmetic and copies ran while one was open for 47% of the time, Pallas kernels for 0%

commit v1 on v0

--- a/solution.py
+++ b/solution.py
@@ -10,6 +10,22 @@
 MOST = 512
 EPS_NORM = 1e-05
 EPS_HEAD = 1e-06
+
+
+def gather_around(x, axis, dim):
+    ways, here, step = (lax.axis_size(axis), lax.axis_index(axis), x.shape[dim])
+    shape = [n * ways if d == dim else n for d, n in enumerate(x.shape)]
+    full = lax.dynamic_update_slice_in_dim(jnp.zeros(shape, x.dtype), x, here * step, axis=dim)
+    going_up = going_down = x
+    for far in range(1, ways // 2 + 1):
+        going_up = lax.ppermute(going_up, axis, [(d, (d + 1) % ways) for d in range(ways)])
+        full = lax.dynamic_update_slice_in_dim(full, going_up, (here - far) % ways * step, axis=dim)
+        if 2 * far < ways:
+            going_down = lax.ppermute(going_down, axis, [(d, (d - 1) % ways) for d in range(ways)])
+            full = lax.dynamic_update_slice_in_dim(
+                full, going_down, (here + far) % ways * step, axis=dim
+            )
+    return full
 
 
 def extended(cells, sides, width, closed):
@@ -85,7 +101,7 @@
         lax.all_gather(own_rows, "tm", axis=1, tiled=True),
     )
     glu_weight, proj_weight = (
-        lax.all_gather(glu_proj, "tm", axis=0, tiled=True),
+        gather_around(glu_proj, "tm", 0),
         lax.all_gather(mix_proj, "tm", axis=0, tiled=True),
     )
     frame_float = frames.astype(jnp.float32)

time: 494 us -> 551 us (1.12)
  starting transfers between devices: 26.2 us -> 75.6 us
  local copies, waits for them, and re-layouts: 100 us -> 114 us
  waiting for transfers between devices: 127 us -> 121 us
    ppermute x0 -> x15, starting transfers between devices: none -> 45.6 us  [the longest x7 24.6 us: gather_around(): lax.ppermute(going_down, axis, [(d, (d - 1) % ways) for d in range(ways)])]
    all_gather x1 -> x0, waiting for transfers between devices: 40.1 us -> none  [on_device(): lax.all_gather(glu_proj, 'tm', axis=0, tiled=True)]
    ppermute x0 -> x15, waiting for transfers between devices: none -> 29.2 us  [the longest x8 29.1 us: gather_around(): lax.ppermute(going_up, axis, [(d, (d + 1) % ways) for d in range(ways)])]
    dynamic_update_slice x0 -> x16, local copies, waits for them, and re-layouts: none -> 11.6 us  [the longest x8 5.78 us: gather_around(): lax.dynamic_update_slice_in_dim(full, going_up, (here - far) % ways * ste...]
    psum x1, waiting for transfers between devices: 31.3 us -> 42.5 us  [on_device(): kernel_sum, gain_sum = lax.psum((kernel_terms, gain_terms), ('head', 'tm'))]
  transfers between devices with their start and end apart: 19 -> 33, of which waited for: 6 -> 11; matrix products, arithmetic and copies ran while one was open for 47% -> 45% of each run, Pallas kernels for 0% -> 0%
where the time goes in v1:
time: 551 us; the launch traced here: 545 us
  waiting for transfers between devices  121 us (22%)
  local copies, waits for them, and re-layouts  114 us (21%)
  other arithmetic  95.4 us (17%)
  starting transfers between devices  75.6 us (14%)
  matrix products  74.2 us (13%)
  blocking collectives  48 us (9%)
  between operations  15.1 us (3%)
    gather x2, local copies, waits for them, and re-layouts, on_device(): conv_segment[window_index] == conv_segment[HALF:HALF + conv_rows][:, None]  55.6 us
    psum x1, blocking collectives, on_device(): kernel_sum, gain_sum = lax.psum((kernel_terms, gain_terms), ('head', 'tm'))  48 us
    all_gather x1, waiting for transfers between devices, on_device(): lax.all_gather(qkv_proj, 'tm', axis=0, tiled=True)  46.5 us
    psum x1, waiting for transfers between devices, on_device(): kernel_sum, gain_sum = lax.psum((kernel_terms, gain_terms), ('head', 'tm'))  42.5 us
    ppermute x8, waiting for transfers between devices, gather_around(): lax.ppermute(going_up, axis, [(d, (d + 1) % ways) for d in range(ways)])  29.1 us
    reduce_sum x6, other arithmetic, on_device(): jnp.sum(depth_float * gated_padded[offset:offset + conv_rows].astype(jnp....  27.5 us
    dot_general x2, matrix products, attend(): jnp.einsum('qhd,khd->hqk', query_rows, key_part, preferred_element_type=j...  26 us
    ppermute x7, starting transfers between devices, gather_around(): lax.ppermute(going_down, axis, [(d, (d - 1) % ways) for d in range(ways)])  24.6 us
  transfers between devices with their start and end apart: 33, of which 11 were waited for; matrix products, arithmetic and copies ran while one was open for 45% of the time, Pallas kernels for 0%

profile of v1, /device:TPU:0, one launch (start us, length us, event | category | flops | bytes accessed | tf_op | source)
XLA Modules:
  0.0 544.6 jit_solution(1991582526244077929)
XLA Ops:
  11.9 46.5 %all-gather.4.cloned.1.call-done = bf16[1024,3,512]{2,0,1:T(8,128)(2,1)} async-done(((bf16[64,3,512]{2,0,1:T(8,128)(2,1)}), bf16[1024,3,512]{2,0,1:T(8,128)(2,1)}) %all-gather.4.cloned.1.call-update) | async-done | bytes 3145744 | tf_op jit(solution)/shard_map/all_gather | solution.py:100
  58.5 4.7 copy.43
  63.2 5.4 fusion.83
  77.2 4.7 fusion.246
  96.5 65.4 %while.12 = (s32[]{:T(128)}, bf16[2,512,512]{2,1,0:T(8,128)(2,1)}, s32[2]{0:T(128)S(1)}, bf16[2048,2,512]{2,0,1:T(8,128)(2,1)}, s32[2048]{0:T(1024)S(1)}, /*inde...) while((s32[]{:T(128)}, bf16[2,512,512]{2,1,0:T(8,128)(2,1)}, ...), condition=%wide.region_8.9_spmd, body=%wide.region_6.8_spmd.sunk | while | flops 1655697408 | bytes 89448936 | solution.py:151
  103.7 13.0 %fusion.267 = (f32[8,512]{1,0:T(8,128)S(1)}, f32[8,512,1536]{2,1,0:T(8,128)}) fusion(f32[8]{0:T(128)S(1)} %bitcast.240, pred[512,1536]{1,0:T(8,128)(4,1)} %broadcast_compare_fusion.2, bf16[1536,8,64]{0,2,1:T(8,128)(2,1)S(1)} %bitcast.131, bf16[1024,8,64]{0,2,1:T(8,128)(2,1)} %get-tuple-element.344, s32[]{:T(128)S(6)} %select_n.250), kind=kOutput, calls=%fused_computation.3.clone.1 | convolution fusion | flops 824176640 | bytes 28065828 | tf_op jit(solution)/shard_map/while/body/eval_jaxpr/qhd,khd->hqk/dot_general | solution.py:136
  116.7 11.2 %fusion.268 = bf16[8,64,512]{2,1,0:T(8,128)(2,1)S(1)} fusion(bf16[1536,8,64]{0,2,1:T(8,128)(2,1)S(1)} %bitcast.130, f32[8,512,1536]{2,1,0:T(8,128)} %get-tuple-element.307, f32[8,512]{1,0:T(8,128)S(1)} %get-tuple-element.308, f32[8]{0:T(128)S(1)} %bitcast.241, pred[512,1536]{1,0:T(8,128)(4,1)S(1)} %copy-done.5), kind=kOutput, calls=%fused_computation.6.clone.1 | convolution fusion | flops 830734336 | bytes 28065824 | tf_op jit(solution)/shard_map/while/body/eval_jaxpr/hqk,khd->qhd/dot_general | solution.py:141
  136.4 13.0 %fusion.267 = (f32[8,512]{1,0:T(8,128)S(1)}, f32[8,512,1536]{2,1,0:T(8,128)}) fusion(f32[8]{0:T(128)S(1)} %bitcast.240, pred[512,1536]{1,0:T(8,128)(4,1)} %broadcast_compare_fusion.2, bf16[1536,8,64]{0,2,1:T(8,128)(2,1)S(1)} %bitcast.131, bf16[1024,8,64]{0,2,1:T(8,128)(2,1)} %get-tuple-element.344, s32[]{:T(128)S(6)} %select_n.250), kind=kOutput, calls=%fused_computation.3.clone.1 | convolution fusion | flops 824176640 | bytes 28065828 | tf_op jit(solution)/shard_map/while/body/eval_jaxpr/qhd,khd->hqk/dot_general | solution.py:136
  149.4 11.2 %fusion.268 = bf16[8,64,512]{2,1,0:T(8,128)(2,1)S(1)} fusion(bf16[1536,8,64]{0,2,1:T(8,128)(2,1)S(1)} %bitcast.130, f32[8,512,1536]{2,1,0:T(8,128)} %get-tuple-element.307, f32[8,512]{1,0:T(8,128)S(1)} %get-tuple-element.308, f32[8]{0:T(128)S(1)} %bitcast.241, pred[512,1536]{1,0:T(8,128)(4,1)S(1)} %copy-done.5), kind=kOutput, calls=%fused_computation.6.clone.1 | convolution fusion | flops 830734336 | bytes 28065824 | tf_op jit(solution)/shard_map/while/body/eval_jaxpr/hqk,khd->qhd/dot_general | solution.py:141
  167.0 18.4 %collective-permute-start.2 = (bf16[64,2048]{1,0:T(8,128)(2,1)S(1)}, bf16[64,2048]{1,0:T(8,128)(2,1)S(1)}, u32[]{:S(2)}, u32[]{:S(2)}) collective-permute-start(bf16[64,2048]{1,0:T(8,128)(2,1)S(1)} %copy-done.16), channel_id=1, source_target_pairs={{0,1},{1,2},{2,3},{3,4},{4,5},{5,6},{6,7},{7,8},{8,9},{9,10},{10,1... | collective-permute-start | bytes 786440 | tf_op jit(solution)/shard_map/ppermute | solution.py:21
  195.9 55.4 %gather_fusion = s32[15872]{0:T(1024)S(1)} fusion(s32[542]{0:T(1024)S(1)} %compare_select_fusion.2, s32[16384]{0:T(1024)S(1)} %pad_clamp_fusion), kind=kCustom, calls=%fused_computation | custom fusion | bytes 190464 | tf_op jit(solution)/shard_map/gather | solution.py:183
  257.7 6.9 %collective-permute-done.4 = bf16[64,2048]{1,0:T(8,128)(2,1)S(1)} collective-permute-done((bf16[64,2048]{1,0:T(8,128)(2,1)S(1)}, bf16[64,2048]{1,0:T(8,128)(2,1)S(1)}, u32[]{:S(2)}, u32[]{:S(2)}) %collective-permute-start.4) | collective-permute-done | bytes 262176 | tf_op jit(solution)/shard_map/ppermute | solution.py:21
  270.5 5.4 collective-permute-done.6
  301.5 4.7 collective-permute-start.15
  311.4 7.0 %collective-permute-done.16 = bf16[64,2048]{1,0:T(8,128)(2,1)S(1)} collective-permute-done((bf16[64,2048]{1,0:T(8,128)(2,1)S(1)}, bf16[64,2048]{1,0:T(8,128)(2,1)S(1)}, u32[]{:S(2)}, u32[]{:S(2)}) %collective-permute-start.16) | collective-permute-done | bytes 262176 | tf_op jit(solution)/shard_map/ppermute | solution.py:21
  341.4 18.6 %fusion.244 = (f32[512]{0:T(512)S(1)}, f32[512,1024]{1,0:T(8,128)S(1)}) fusion(f32[512]{0:T(512)S(1)} %get-tuple-element.160, bf16[15,1024]{1,0:T(8,128)(2,1)S(1)} %broadcast_select_fusion.1, bf16[512,1024]{1,0:T(8,128)(2,1)S(1)} %multiply_convert_fusion.6, f32[1024]{0:T(1024)S(1)} %bitcast.163, f32[512]{0:T(512)S(1)} %get-tuple-element.161, ...), kind=kLoop, calls=%fused_computation.499 | loop fusion | flops 112197120 | bytes 3399680 | tf_op jit(solution)/shard_map/reduce_sum | solution.py:49
  360.5 5.0 multiply_reduce_fusion.1
  365.6 7.3 %fusion.160 = (f32[1024]{0:T(1024)}, f32[1024]{0:T(1024)}, f32[1024]{0:T(1024)}, f32[1024]{0:T(1024)}, f32[1024]{0:T(1024)}, /*index=5*/f32[1024]{0:T(1024)}, bf16[512,1024]{1,0:T(8,128)(2,1)S(1)}) fusion(f32[512]{0:T(512)S(1)} %get-tuple-element.161, bf16[15,1024]{1,0:T(8,128)(2,1)S(1)} %broadcast_select_fusion.1, ...), kind=kLoop, calls=%fused_computation.293 | loop fusion | flops 26732544 | bytes 6371328 | tf_op jit(solution)/shard_map/reduce_sum | solution.py:214
  380.8 7.1 %fusion.162 = (f32[1024]{0:T(1024)}, f32[1024]{0:T(1024)}, f32[1024]{0:T(1024)}, f32[1024]{0:T(1024)}, f32[1024]{0:T(1024)}, /*index=5*/f32[1024]{0:T(1024)}) fusion(bf16[512,1024]{1,0:T(8,128)(2,1)S(1)} %get-tuple-element.204, bf16[15,1024]{1,0:T(8,128)(2,1)S(1)} %broadcast_select_fusion.1, bf16[512,1024]{1,0:T(8,128)(2,1)S(1)} %multiply_convert_fusion.6, ...), kind=kLoop, calls=%fused_computation.295 | loop fusion | flops 22538240 | bytes 2164736 | tf_op jit(solution)/shard_map/reduce_sum | solution.py:214
  402.9 5.5 %stack.144 = f32[31,1024]{1,0:T(8,128)} concatenate(f32[1,1024]{1,0:T(1,128)} %bitcast.216, f32[1,1024]{1,0:T(1,128)} %bitcast.235, f32[1,1024]{1,0:T(1,128)} %bitcast.234, f32[1,1024]{1,0:T(1,128)} %bitcast.233, f32[1,1024]{1,0:T(1,128)} %bitcast.218, f32[1,1024]{1,0:T(1,128)} %bitcast.219, f32[1,1024]{1,0:T(1,128)} %bitcast.220, f32[1,1024]{1,0:T(1,128)} %bitcast.221, ...), dimensions={0} | concatenate | bytes 253952 | tf_op jit(solution)/shard_map/stack | solution.py:212
  412.3 19.3 %multiply_convert_fusion.3 = (bf16[512,1024]{1,0:T(8,128)(2,1)S(1)}, f32[512,1024]{1,0:T(8,128)S(1)}) fusion(f32[512,2048]{1,0:T(8,128)} %copy-done.3, f32[512]{0:T(512)S(1)} %get-tuple-element.160, bf16[15,1024]{1,0:T(8,128)(2,1)S(1)} %broadcast_select_fusion, bf16[512,1024]{1,0:T(8,128)(2,1)S(1)} %get-tuple-element.204, f32[1024]{0:T(1024)S(1)} %bitcast.168, ...), kind=kLoop, calls=%fused_computation.310 | loop fusion | flops 114294784 | bytes 6543360 | tf_op jit(solution)/shard_map/convert
  432.5 5.1 fusion.19
  443.2 48.0 %psum.15 = f32[2,1024]{1,0:T(2,128)S(1)} all-reduce(f32[2,1024]{1,0:T(2,128)S(1)} %pad_maximum_fusion.6), channel_id=1, replica_groups=mesh['head'=2,'tm'=16] {'head','tm'}, use_global_device_ids=true, to_apply=%region_53.54 | all-reduce | flops 2048 | bytes 16384 | tf_op jit(solution)/shard_map/psum | solution.py:234
  491.8 42.5 %all-reduce.2.cloned.1.call-done = f32[31,1024]{1,0:T(8,128)} async-done(((f32[31,1024]{1,0:T(8,128)}), f32[31,1024]{1,0:T(8,128)}) %all-reduce.2.cloned.1.call-update) | async-done | bytes 126992 | tf_op jit(solution)/shard_map/psum | solution.py:234
  (284 shorter events, 162.0 us)
Async XLA Ops:
  7.2 51.3 %all-gather.4.cloned.1.call-start = ((), (), s32[]{:S(2)}) async-start(), calls=%async_computation.4 | async-start | bytes 3342336 | tf_op jit(solution)/shard_map/all_gather | solution.py:100
  7.9 154.0 %all-gather.6.cloned.1.call-start = ((), (), s32[]{:S(2)}) async-start(), calls=%async_computation.5 | async-start | bytes 1114112 | tf_op jit(solution)/shard_map/all_gather | solution.py:101
  8.7 310.4 %reduce-scatter.2.cloned.1.call-start = ((), (), s32[]{:S(2)}) async-start(), calls=%async_computation.6 | async-start | bytes 3145728 | tf_op jit(solution)/shard_map/reduce_scatter | solution.py:154
  83.4 9.7 %collective-permute-start.1 = (bf16[512,2,512]{2,0,1:T(8,128)(2,1)}, bf16[512,2,512]{2,0,1:T(8,128)(2,1)}, u32[]{:S(2)}, u32[]{:S(2)}) collective-permute-start(bf16[512,2,512]{2,0,1:T(8,128)(2,1)} %get-tuple-element.218), channel_id=1, source_target_pairs={{1,0},{2,1},{3,2},{4,3},{5,4},{6,5},{7,6},{8,7},{9,8},{10,9},{11,1... | collective-permute-start | bytes 3145736 | tf_op jit(solution)/shard_map/ppermute | solution.py:41
  167.0 84.8 %collective-permute-start.2 = (bf16[64,2048]{1,0:T(8,128)(2,1)S(1)}, bf16[64,2048]{1,0:T(8,128)(2,1)S(1)}, u32[]{:S(2)}, u32[]{:S(2)}) collective-permute-start(bf16[64,2048]{1,0:T(8,128)(2,1)S(1)} %copy-done.16), channel_id=1, source_target_pairs={{0,1},{1,2},{2,3},{3,4},{4,5},{5,6},{6,7},{7,8},{8,9},{9,10},{10,1... | collective-permute-start | bytes 786440 | tf_op jit(solution)/shard_map/ppermute | solution.py:21
  185.4 69.0 %collective-permute-start.3 = (bf16[64,2048]{1,0:T(8,128)(2,1)S(1)}, bf16[64,2048]{1,0:T(8,128)(2,1)S(1)}, u32[]{:S(2)}, u32[]{:S(2)}) collective-permute-start(bf16[64,2048]{1,0:T(8,128)(2,1)S(1)} %copy-done.16), channel_id=1, source_target_pairs={{0,15},{1,0},{2,1},{3,2},{4,3},{5,4},{6,5},{7,6},{8,7},{9,8},{10,9... | collective-permute-start | bytes 786440 | tf_op jit(solution)/shard_map/ppermute | solution.py:24
  185.4 151.1 %all-to-all-start.1 = ((bf16[2,512,512]{2,1,0:T(8,128)(2,1)}), bf16[2,512,512]{2,1,0:T(8,128)(2,1)S(1)}, u32[]{:S(2)}, u32[]{:S(2)}) async-start(bf16[2,512,512]{2,1,0:T(8,128)(2,1)} %bitcast.48), calls=%async_computation.2 | async-start | bytes 2097152 | tf_op jit(solution)/shard_map/all_to_all | solution.py:206
  188.9 171.6 %all-gather.8.cloned.1.call-start = ((), (), s32[]{:S(2)}) async-start(), calls=%async_computation.7 | async-start | bytes 2228224 | tf_op jit(solution)/shard_map/all_gather | solution.py:105
  251.8 12.9 %collective-permute-start.4 = (bf16[64,2048]{1,0:T(8,128)(2,1)S(1)}, bf16[64,2048]{1,0:T(8,128)(2,1)S(1)}, u32[]{:S(2)}, u32[]{:S(2)}) collective-permute-start(bf16[64,2048]{1,0:T(8,128)(2,1)S(1)} %collective-permute-done.2), channel_id=1, source_target_pairs={{0,1},{1,2},{2,3},{3,4},{4,5},{5,6},{6,7},{7,8},{8,9},{9,10},{10,1... | collective-permute-start | bytes 786440 | tf_op jit(solution)/shard_map/ppermute | solution.py:21
  254.4 10.2 %collective-permute-start.5 = (bf16[64,2048]{1,0:T(8,128)(2,1)S(1)}, bf16[64,2048]{1,0:T(8,128)(2,1)S(1)}, u32[]{:S(2)}, u32[]{:S(2)}) collective-permute-start(bf16[64,2048]{1,0:T(8,128)(2,1)S(1)} %collective-permute-done.3), channel_id=1, source_target_pairs={{0,15},{1,0},{2,1},{3,2},{4,3},{5,4},{6,5},{7,6},{8,7},{9,8},{10,9... | collective-permute-start | bytes 786440 | tf_op jit(solution)/shard_map/ppermute | solution.py:24
  264.6 11.3 %collective-permute-start.6 = (bf16[64,2048]{1,0:T(8,128)(2,1)S(1)}, bf16[64,2048]{1,0:T(8,128)(2,1)S(1)}, u32[]{:S(2)}, u32[]{:S(2)}) collective-permute-start(bf16[64,2048]{1,0:T(8,128)(2,1)S(1)} %collective-permute-done.4), channel_id=1, source_target_pairs={{0,1},{1,2},{2,3},{3,4},{4,5},{5,6},{6,7},{7,8},{8,9},{9,10},{10,1... | collective-permute-start | bytes 786440 | tf_op jit(solution)/shard_map/ppermute | solution.py:21
  264.6 11.3 %collective-permute-start.7 = (bf16[64,2048]{1,0:T(8,128)(2,1)S(1)}, bf16[64,2048]{1,0:T(8,128)(2,1)S(1)}, u32[]{:S(2)}, u32[]{:S(2)}) collective-permute-start(bf16[64,2048]{1,0:T(8,128)(2,1)S(1)} %collective-permute-done.5), channel_id=1, source_target_pairs={{0,15},{1,0},{2,1},{3,2},{4,3},{5,4},{6,5},{7,6},{8,7},{9,8},{10,9... | collective-permute-start | bytes 786440 | tf_op jit(solution)/shard_map/ppermute | solution.py:24
  275.9 8.5 %collective-permute-start.8 = (bf16[64,2048]{1,0:T(8,128)(2,1)S(1)}, bf16[64,2048]{1,0:T(8,128)(2,1)S(1)}, u32[]{:S(2)}, u32[]{:S(2)}) collective-permute-start(bf16[64,2048]{1,0:T(8,128)(2,1)S(1)} %collective-permute-done.6), channel_id=1, source_target_pairs={{0,1},{1,2},{2,3},{3,4},{4,5},{5,6},{6,7},{7,8},{8,9},{9,10},{10,1... | collective-permute-start | bytes 786440 | tf_op jit(solution)/shard_map/ppermute | solution.py:21
  275.9 8.5 %collective-permute-start.9 = (bf16[64,2048]{1,0:T(8,128)(2,1)S(1)}, bf16[64,2048]{1,0:T(8,128)(2,1)S(1)}, u32[]{:S(2)}, u32[]{:S(2)}) collective-permute-start(bf16[64,2048]{1,0:T(8,128)(2,1)S(1)} %collective-permute-done.7), channel_id=1, source_target_pairs={{0,15},{1,0},{2,1},{3,2},{4,3},{5,4},{6,5},{7,6},{8,7},{9,8},{10,9... | collective-permute-start | bytes 786440 | tf_op jit(solution)/shard_map/ppermute | solution.py:24
  284.4 8.5 %collective-permute-start.10 = (bf16[64,2048]{1,0:T(8,128)(2,1)S(1)}, bf16[64,2048]{1,0:T(8,128)(2,1)S(1)}, u32[]{:S(2)}, u32[]{:S(2)}) collective-permute-start(bf16[64,2048]{1,0:T(8,128)(2,1)S(1)} %collective-permute-done.8), channel_id=1, source_target_pairs={{0,1},{1,2},{2,3},{3,4},{4,5},{5,6},{6,7},{7,8},{8,9},{9,10},{10,1... | collective-permute-start | bytes 786440 | tf_op jit(solution)/shard_map/ppermute | solution.py:21
  284.4 8.5 %collective-permute-start.11 = (bf16[64,2048]{1,0:T(8,128)(2,1)S(1)}, bf16[64,2048]{1,0:T(8,128)(2,1)S(1)}, u32[]{:S(2)}, u32[]{:S(2)}) collective-permute-start(bf16[64,2048]{1,0:T(8,128)(2,1)S(1)} %collective-permute-done.9), channel_id=1, source_target_pairs={{0,15},{1,0},{2,1},{3,2},{4,3},{5,4},{6,5},{7,6},{8,7},{9,8},{10,9... | collective-permute-start | bytes 786440 | tf_op jit(solution)/shard_map/ppermute | solution.py:24
  292.9 8.5 %collective-permute-start.12 = (bf16[64,2048]{1,0:T(8,128)(2,1)S(1)}, bf16[64,2048]{1,0:T(8,128)(2,1)S(1)}, u32[]{:S(2)}, u32[]{:S(2)}) collective-permute-start(bf16[64,2048]{1,0:T(8,128)(2,1)S(1)} %collective-permute-done.10), channel_id=1, source_target_pairs={{0,1},{1,2},{2,3},{3,4},{4,5},{5,6},{6,7},{7,8},{8,9},{9,10},{10,1... | collective-permute-start | bytes 786440 | tf_op jit(solution)/shard_map/ppermute | solution.py:21
  292.9 8.5 %collective-permute-start.13 = (bf16[64,2048]{1,0:T(8,128)(2,1)S(1)}, bf16[64,2048]{1,0:T(8,128)(2,1)S(1)}, u32[]{:S(2)}, u32[]{:S(2)}) collective-permute-start(bf16[64,2048]{1,0:T(8,128)(2,1)S(1)} %collective-permute-done.11), channel_id=1, source_target_pairs={{0,15},{1,0},{2,1},{3,2},{4,3},{5,4},{6,5},{7,6},{8,7},{9,8},{10,9... | collective-permute-start | bytes 786440 | tf_op jit(solution)/shard_map/ppermute | solution.py:24
  301.5 9.2 %collective-permute-start.15 = (bf16[64,2048]{1,0:T(8,128)(2,1)S(1)}, bf16[64,2048]{1,0:T(8,128)(2,1)S(1)}, u32[]{:S(2)}, u32[]{:S(2)}) collective-permute-start(bf16[64,2048]{1,0:T(8,128)(2,1)S(1)} %collective-permute-done.13), channel_id=1, source_target_pairs={{0,15},{1,0},{2,1},{3,2},{4,3},{5,4},{6,5},{7,6},{8,7},{9,8},{10,9... | collective-permute-start | bytes 786440 | tf_op jit(solution)/shard_map/ppermute | solution.py:24
  389.9 18.5 %collective-permute-start.21 = (bf16[15,1024]{1,0:T(8,128)(2,1)S(1)}, bf16[15,1024]{1,0:T(8,128)(2,1)S(1)}, u32[]{:S(2)}, u32[]{:S(2)}) collective-permute-start(bf16[15,1024]{1,0:T(8,128)(2,1)S(1)} %get-tuple-element.219), channel_id=1, source_target_pairs={{0,16},{16,0},{1,17},{17,1},{2,18},{18,2},{3,19},{19,3},{4,20},{20... | collective-permute-start | bytes 92168 | tf_op jit(solution)/shard_map/ppermute | solution.py:39
  394.7 16.8 %collective-permute-start.24 = (bf16[15,1024]{1,0:T(8,128)(2,1)S(1)}, bf16[15,1024]{1,0:T(8,128)(2,1)S(1)}, u32[]{:S(2)}, u32[]{:S(2)}) collective-permute-start(bf16[15,1024]{1,0:T(8,128)(2,1)S(1)} %collective-permute-done.23), channel_id=1, source_target_pairs={{1,0},{2,1},{3,2},{4,3},{5,4},{6,5},{7,6},{8,7},{9,8},{10,9},{11,1... | collective-permute-start | bytes 92168 | tf_op jit(solution)/shard_map/ppermute | solution.py:41
  399.1 40.4 %all-to-all-start = ((bf16[512,2,512]{2,0,1:T(8,128)(2,1)}), bf16[512,2,512]{2,0,1:T(8,128)(2,1)S(1)}, u32[]{:S(2)}, u32[]{:S(2)}) async-start(bf16[512,2,512]{2,0,1:T(8,128)(2,1)} %bitcast.136), calls=%async_computation.1 | async-start | bytes 2097152 | tf_op jit(solution)/shard_map/all_to_all | solution.py:205
  402.7 131.6 %all-reduce.2.cloned.1.call-start = ((), (), s32[]{:S(2)}) async-start(), calls=%async_computation.8 | async-start | bytes 262144 | tf_op jit(solution)/shard_map/psum | solution.py:234
  439.5 96.4 %all-to-all-start.2 = ((bf16[512,2,512]{2,0,1:T(8,128)(2,1)}), bf16[512,2,512]{2,0,1:T(8,128)(2,1)S(1)}, u32[]{:S(2)}, u32[]{:S(2)}) async-start(bf16[512,2,512]{2,0,1:T(8,128)(2,1)} %bitcast.114), calls=%async_computation.3 | async-start | bytes 2097152 | tf_op jit(solution)/shard_map/all_to_all | solution.py:236
  (64 other events, 601.4 us)
Sparse Core Ops, SparseCore 0:
  10.2 48.2 all-gather.3
  61.2 36.6 all-gather.5
  166.2 61.4 reduce-scatter.1
  229.7 44.7 all-gather.7
  409.3 124.9 all-reduce.1
